TPU v7x, 32 devices: a whole 2x2x4 slice. The times are simulated.
32 devices in a mesh: shard: 2 (over y), ctx: 4 (over z), tp: 4 (over x, core).
Axes of the slice: x: 2, y: 2, z: 4, core: 2. Of those that a mesh axis runs over, the one named last changes fastest.
Arguments:
- x_in: float32 [4096, 768], P(('shard', 'ctx')), may hold values from -6 to 6
- norm_gain: bfloat16 [768], P(('shard', 'ctx')), may hold values from 0.5 to 1.5
- w_z: bfloat16 [768, 1536], P(('shard', 'ctx'), 'tp'), may hold values from -0.21875 to 0.21875
- w_x: bfloat16 [768, 1536], P(('shard', 'ctx'), 'tp'), may hold values from -0.21875 to 0.21875
- w_bc: bfloat16 [768, 256], P(('shard', 'ctx')), may hold values from -0.21875 to 0.21875
- w_dt: bfloat16 [768, 24], P(('shard', 'ctx'), 'tp'), may hold values from -0.21875 to 0.21875
- w_out: bfloat16 [768, 1536], P(('shard', 'ctx'), 'tp'), may hold values from -0.15625 to 0.15625
- conv_wx: float32 [4, 1536], P(None, 'tp'), may hold values from -3 to 3
- conv_bx: float32 [1536], P('tp'), may hold values from -0.5 to 0.5
- conv_wbc: float32 [4, 256], replicated, may hold values from -3 to 3
- conv_bbc: float32 [256], replicated, may hold values from -0.5 to 0.5
- dt_bias: float32 [24], P('tp'), may hold values from -6 to -3
- a_log: float32 [24], P('tp'), may hold values from -6 to 2
- d_skip: float32 [24], P('tp'), may hold values from 0.5 to 1.5
- gate_gain: float32 [1536], P('tp'), may hold values from 0.5 to 1.5
- seq_lens: int32 [2, 3], P('shard'), may hold values from 1 to 1280, 2048 in all within a row
- token_mask: int32 [4096], P(('shard', 'ctx')), may hold values 0 or 1
- d_out: float32 [4096, 768], P(('shard', 'ctx')), may hold values from -6 to 6
Outputs:
- block_out: float32 [4096, 768], P(('shard', 'ctx'))
- d_x: float32 [4096, 768], P(('shard', 'ctx'))
- d_norm_gain: float32 [768], P(('shard', 'ctx'))
- d_w_z: float32 [768, 1536], P(('shard', 'ctx'), 'tp')
- d_w_x: float32 [768, 1536], P(('shard', 'ctx'), 'tp')
- d_w_bc: float32 [768, 256], P(('shard', 'ctx'))
- d_w_dt: float32 [768, 24], P(('shard', 'ctx'), 'tp')
- d_w_out: float32 [768, 1536], P(('shard', 'ctx'), 'tp')
- d_conv_wx: float32 [4, 1536], P(None, 'tp')
- d_conv_bx: float32 [1536], P('tp')
- d_conv_wbc: float32 [4, 256], replicated
- d_conv_bbc: float32 [256], replicated
- d_dt_bias: float32 [24], P('tp')
- d_a_log: float32 [24], P('tp')
- d_d_skip: float32 [24], P('tp')
- d_gate_gain: float32 [1536], P('tp')
Inputs may be any that keep to these rules, and one draw needn't show every extreme that they name: `seq_lens`: each row sums to 2048, and its longest sequence has exactly 1280 positions.
All inputs are finite; a program needn't handle non-finite values. No bound on the sum of `token_mask` on one device may be relied on, other than what follows from the above.
Results may differ from a plain program's by a relative error of at most 0.014.
Values may be sent and summed in bfloat16 or wider, within the bound.
No kernel may reach another device: no remote copies, remote signals or barrier semaphores. Data moves between devices by JAX's collectives and lax.ppermute only.
A program may use at most 128 MiB of HBM per device.

v0:
```python
import jax
import jax.numpy as jnp
from jax import lax
from jax.sharding import PartitionSpec as P

SPAN = 256
norm_eps = 1e-05


def passed_along(value, axis, steps):
    count = lax.axis_size(axis)
    initial, last = (max(0, -steps), min(count, count - steps))
    return lax.ppermute(value, axis, [(source, source + steps) for source in range(initial, last)])


def entering_2(part, axis, combine, identity, reverse):
    count = lax.axis_size(axis)
    place = lax.axis_index(axis)
    ahead = count - 1 - place if reverse else place
    gathered = jax.tree.map(lambda a: lax.all_gather(a, axis), part)
    state = jax.tree.map(lambda a, e: jnp.zeros_like(a) + jnp.asarray(e, a.dtype), part, identity)

    def one(step, state):
        source = count - 1 - step if reverse else step
        return combine(
            state, jax.tree.map(lambda a: lax.dynamic_index_in_dim(a, source, 0, False), gathered)
        )

    return lax.fori_loop(0, ahead, one, state)


def segment_ids(positions, lengths_row):
    bounds = jnp.cumsum(lengths_row)
    counted = jnp.sum((positions[:, None] >= bounds[None, :]).astype(jnp.int32), axis=1)
    return jnp.where(positions < 0, -1, counted)


def conv_silu(extended, seg_ext, weight, conv_bias):
    width_taps = weight.shape[0]
    row_count = extended.shape[0] - (width_taps - 1)
    summed = jnp.zeros((row_count, extended.shape[1]), jnp.float32) + conv_bias[None, :]
    for offset in range(width_taps):
        same_doc = (seg_ext[offset : offset + row_count] == seg_ext[width_taps - 1 :]).astype(
            jnp.float32
        )
        summed = (
            summed
            + weight[offset][None, :] * extended[offset : offset + row_count] * same_doc[:, None]
        )
    return jax.nn.silu(summed)


def span_output(ssm_in, step_size, decay_rate, b_state, c_state, segment, seg_prev, state_in):
    cumulated = jnp.cumsum(step_size * decay_rate[None, :], axis=0)
    length = ssm_in.shape[0]
    ordering = jnp.arange(length, dtype=jnp.int32)
    allowed = (segment[:, None] == segment[None, :]) & (ordering[:, None] >= ordering[None, :])
    log_gaps = cumulated[:, None, :] - cumulated[None, :, :]
    log_gaps = jnp.where(allowed[:, :, None], log_gaps, 0.0)
    decays = jnp.where(allowed[:, :, None], jnp.exp(log_gaps), 0.0)
    scores = lax.dot_general(
        c_state, b_state, (((1,), (1,)), ((), ())), precision=lax.Precision.HIGHEST
    )
    mixing = scores[:, :, None] * decays * step_size[None, :, :]
    within = jnp.einsum("tsh,shp->thp", mixing, ssm_in, precision=lax.Precision.HIGHEST)
    carried = jnp.einsum("tn,hpn->thp", c_state, state_in, precision=lax.Precision.HIGHEST)
    entering = jnp.exp(cumulated) * (segment == seg_prev).astype(jnp.float32)[:, None]
    return within + carried * entering[:, :, None]


def span_state(ssm_in, step_size, decay_rate, b_state, segment, seg_prev):
    cumulated = jnp.cumsum(step_size * decay_rate[None, :], axis=0)
    final_sum = cumulated[-1]
    kept = (segment == segment[-1])[:, None]
    remaining = jnp.where(kept, final_sum[None, :] - cumulated, 0.0)
    weighting = jnp.where(kept, jnp.exp(remaining) * step_size, 0.0)
    scaled_in = ssm_in * weighting[:, :, None]
    state_out = jnp.einsum("shp,sn->hpn", scaled_in, b_state, precision=lax.Precision.HIGHEST)
    passing = jnp.exp(final_sum) * (segment[-1] == seg_prev).astype(jnp.float32)
    return (passing, state_out)


def forward_join(earlier, later):
    return (earlier[0] * later[0], later[0][:, None, None] * earlier[1] + later[1])


def backward_join(earlier, later):
    return (earlier[0] * later[0], later[1] + later[0][:, None, None] * earlier[1])


def contract_rows(left_side, right_side):
    return lax.dot_general(
        left_side, right_side, (((0,), (0,)), ((), ())), preferred_element_type=jnp.float32
    )


def contract_cols(left_side, right_side):
    return lax.dot_general(
        left_side, right_side, (((1,), (1,)), ((), ())), preferred_element_type=jnp.float32
    )


def local(
    x_in,
    norm_gain,
    w_z,
    w_x,
    w_bc,
    w_dt,
    w_out,
    conv_wx,
    conv_bx,
    conv_wbc,
    conv_bbc,
    dt_bias,
    a_log,
    d_skip,
    gate_gain,
    seq_lens,
    token_mask,
    d_out,
):
    row_count = x_in.shape[0]
    head_count = dt_bias.shape[0]
    inner_local = w_z.shape[1]
    head_width = inner_local // head_count
    state_width = w_bc.shape[1] // 2
    edge_rows = conv_wx.shape[0] - 1
    span_count = row_count // SPAN
    tp_count = lax.axis_size("tp")
    inner_total = inner_local * tp_count
    gathered = (
        lax.all_gather(norm_gain, ("shard", "ctx"), axis=0, tiled=True),
        lax.all_gather(w_z, ("shard", "ctx"), axis=0, tiled=True),
        lax.all_gather(w_x, ("shard", "ctx"), axis=0, tiled=True),
        lax.all_gather(w_bc, ("shard", "ctx"), axis=0, tiled=True),
        lax.all_gather(w_dt, ("shard", "ctx"), axis=0, tiled=True),
        lax.all_gather(w_out, ("shard", "ctx"), axis=0, tiled=True),
    )
    gain_all, wz_all, wx_all, wbc_all, wdt_all, wout_all = gathered
    inv_rms = lax.rsqrt(jnp.mean(x_in * x_in, axis=1, keepdims=True) + norm_eps)
    normed = (x_in * inv_rms * gain_all[None, :]).astype(jnp.bfloat16)
    proj_z = jnp.dot(normed, wz_all, preferred_element_type=jnp.float32).astype(jnp.bfloat16)
    proj_x = jnp.dot(normed, wx_all, preferred_element_type=jnp.float32).astype(jnp.bfloat16)
    proj_bc = jnp.dot(normed, wbc_all, preferred_element_type=jnp.float32).astype(jnp.bfloat16)
    proj_dt = jnp.dot(normed, wdt_all, preferred_element_type=jnp.float32).astype(jnp.bfloat16)
    conv_input = jnp.concatenate([proj_x, proj_bc], axis=1)
    edge_in = passed_along(conv_input[row_count - edge_rows :], "ctx", 1)
    extended = jnp.concatenate([edge_in, conv_input], axis=0).astype(jnp.float32)
    positions = lax.axis_index("ctx") * row_count + jnp.arange(
        -edge_rows, row_count, dtype=jnp.int32
    )
    seg_ext = segment_ids(positions, seq_lens[0])
    segment = seg_ext[edge_rows:]
    seg_prev = seg_ext[edge_rows - 1 : edge_rows - 1 + row_count : SPAN]
    conv_w = jnp.concatenate([conv_wx, conv_wbc], axis=1)
    conv_b = jnp.concatenate([conv_bx, conv_bbc])

    def conv_piece(ext_arg, weight_arg, bias_arg):
        return conv_silu(ext_arg, seg_ext, weight_arg, bias_arg)

    activated, conv_back = jax.vjp(conv_piece, extended, conv_w, conv_b)
    ssm_in = activated[:, :inner_local].reshape(row_count, head_count, head_width)
    b_state = activated[:, inner_local : inner_local + state_width]
    c_state = activated[:, inner_local + state_width :]
    mask_f = token_mask.astype(jnp.float32)
    dt_pre = proj_dt.astype(jnp.float32) + dt_bias[None, :]
    step_size = jax.nn.softplus(dt_pre) * mask_f[:, None]
    decay_rate = -jnp.exp(a_log)
    span_in = ssm_in.reshape(span_count, SPAN, head_count, head_width)
    span_dt = step_size.reshape(span_count, SPAN, head_count)
    span_b = b_state.reshape(span_count, SPAN, state_width)
    span_c = c_state.reshape(span_count, SPAN, state_width)
    span_seg = segment.reshape(span_count, SPAN)

    def states_call(in_arg, dt_arg, rate_arg, b_arg):
        return jax.vmap(span_state, in_axes=(0, 0, None, 0, 0, 0))(
            in_arg, dt_arg, rate_arg, b_arg, span_seg, seg_prev
        )

    (passing, local_states), state_back = jax.vjp(states_call, span_in, span_dt, decay_rate, span_b)
    ones_head = jnp.ones((head_count,), jnp.float32)
    zeros_state = jnp.zeros((head_count, head_width, state_width), jnp.float32)
    dev_pass, dev_state = (ones_head, zeros_state)
    for span_index in range(span_count):
        dev_pass, dev_state = forward_join(
            (dev_pass, dev_state), (passing[span_index], local_states[span_index])
        )
    state_entry = entering_2(
        (dev_pass, dev_state), "ctx", forward_join, (ones_head, zeros_state), False
    )[1]
    entries = []
    current = state_entry
    for span_index in range(span_count):
        entries.append(current)
        current = passing[span_index][:, None, None] * current + local_states[span_index]
    span_entry = jnp.stack(entries)

    def outputs_call(in_arg, dt_arg, rate_arg, b_arg, c_arg, entry_arg):
        return jax.vmap(span_output, in_axes=(0, 0, None, 0, 0, 0, 0, 0))(
            in_arg, dt_arg, rate_arg, b_arg, c_arg, span_seg, seg_prev, entry_arg
        )

    span_out, output_back = jax.vjp(
        outputs_call, span_in, span_dt, decay_rate, span_b, span_c, span_entry
    )
    ssm_out = span_out.reshape(row_count, head_count, head_width) + d_skip[None, :, None] * ssm_in
    ssm_flat = ssm_out.reshape(row_count, inner_local)
    z_float = proj_z.astype(jnp.float32)
    gate_act = jax.nn.silu(z_float)
    gated = ssm_flat * gate_act
    square_sum = lax.psum(jnp.sum(gated * gated, axis=1), "tp")
    inv_gate = lax.rsqrt(square_sum / inner_total + norm_eps)
    mixed = (gated * inv_gate[:, None] * gate_gain[None, :]).astype(jnp.bfloat16)
    block_out = x_in + lax.psum(contract_cols(mixed, wout_all), "tp")
    weights_back = (
        lax.all_gather(norm_gain, ("shard", "ctx"), axis=0, tiled=True),
        lax.all_gather(w_z, ("shard", "ctx"), axis=0, tiled=True),
        lax.all_gather(w_x, ("shard", "ctx"), axis=0, tiled=True),
        lax.all_gather(w_bc, ("shard", "ctx"), axis=0, tiled=True),
        lax.all_gather(w_dt, ("shard", "ctx"), axis=0, tiled=True),
        lax.all_gather(w_out, ("shard", "ctx"), axis=0, tiled=True),
    )
    gain_back, wz_back, wx_back, wbc_back, wdt_back, wout_back = weights_back
    grad_low = d_out.astype(jnp.bfloat16)
    d_mixed = jnp.dot(grad_low, wout_back, preferred_element_type=jnp.float32)
    d_w_out = contract_rows(grad_low, mixed)
    scaled = d_mixed * gate_gain[None, :]
    back_dot = lax.psum(jnp.sum(scaled * gated, axis=1), "tp")
    d_gated = (
        scaled * inv_gate[:, None]
        - gated * (inv_gate * inv_gate * inv_gate * back_dot / inner_total)[:, None]
    )
    d_gate_gain = jnp.sum(d_mixed * gated * inv_gate[:, None], axis=0)
    sigmoid_z = jax.nn.sigmoid(z_float)
    d_z = d_gated * ssm_flat * sigmoid_z * (1.0 + z_float * (1.0 - sigmoid_z))
    d_ssm = (d_gated * gate_act).reshape(row_count, head_count, head_width)
    d_d_skip = jnp.sum(d_ssm * ssm_in, axis=(0, 2))
    g_in, g_dt, g_rate, g_b, g_c, g_entry = output_back(
        d_ssm.reshape(span_count, SPAN, head_count, head_width)
    )
    back_pass, back_grad = (ones_head, zeros_state)
    for span_index in reversed(range(span_count)):
        back_pass, back_grad = backward_join(
            (back_pass, back_grad), (passing[span_index], g_entry[span_index])
        )
    exit_grad = entering_2(
        (back_pass, back_grad), "ctx", backward_join, (ones_head, zeros_state), True
    )[1]
    next_grad = exit_grad
    pass_list = []
    state_list = []
    for span_index in reversed(range(span_count)):
        pass_list.append(jnp.sum(next_grad * span_entry[span_index], axis=(1, 2)))
        state_list.append(next_grad)
        next_grad = g_entry[span_index] + passing[span_index][:, None, None] * next_grad
    s_in, s_dt, s_rate, s_b = state_back((jnp.stack(pass_list[::-1]), jnp.stack(state_list[::-1])))
    d_in_total = (
        d_ssm * d_skip[None, :, None] + (g_in + s_in).reshape(row_count, head_count, head_width)
    ).reshape(row_count, inner_local)
    d_step = (g_dt + s_dt).reshape(row_count, head_count)
    d_a_log = (g_rate + s_rate) * decay_rate
    d_dt_pre = d_step * mask_f[:, None] * jax.nn.sigmoid(dt_pre)
    d_dt_bias = jnp.sum(d_dt_pre, axis=0)
    d_bc = lax.psum(
        jnp.concatenate(
            [(g_b + s_b).reshape(row_count, state_width), g_c.reshape(row_count, state_width)],
            axis=1,
        ),
        "tp",
    )
    d_ext, d_conv_w, d_conv_b = conv_back(jnp.concatenate([d_in_total, d_bc], axis=1))
    edge_grad = passed_along(d_ext[:edge_rows], "ctx", -1)
    d_conv_in = d_ext[edge_rows:] + jnp.concatenate(
        [jnp.zeros((row_count - edge_rows, d_ext.shape[1]), jnp.float32), edge_grad], axis=0
    )
    d_proj_z = d_z.astype(jnp.bfloat16)
    d_proj_x = d_conv_in[:, :inner_local].astype(jnp.bfloat16)
    d_proj_bc = d_conv_in[:, inner_local:].astype(jnp.bfloat16)
    d_proj_dt = d_dt_pre.astype(jnp.bfloat16)
    d_w_z = contract_rows(normed, d_proj_z)
    d_w_x = contract_rows(normed, d_proj_x)
    d_w_bc = contract_rows(normed, d_proj_bc)
    d_w_dt = contract_rows(normed, d_proj_dt)
    share = 2 * state_width // tp_count
    share_start = lax.axis_index("tp") * share
    bc_part = lax.dynamic_slice_in_dim(d_proj_bc, share_start, share, 1)
    wbc_part = lax.dynamic_slice_in_dim(wbc_back, share_start, share, 1)
    d_normed_part = (
        contract_cols(d_proj_z, wz_back)
        + contract_cols(d_proj_x, wx_back)
        + contract_cols(d_proj_dt, wdt_back)
        + contract_cols(bc_part, wbc_part)
    )
    d_normed = lax.psum(d_normed_part, "tp")
    gain_float = gain_back.astype(jnp.float32)
    weighted = d_normed * gain_float[None, :]
    row_dot = jnp.sum(weighted * x_in, axis=1, keepdims=True)
    d_input = (
        d_out + weighted * inv_rms - x_in * (inv_rms * inv_rms * inv_rms) * row_dot / x_in.shape[1]
    )
    d_norm_gain = jnp.sum(d_normed * x_in * inv_rms, axis=0)
    grads_rows = (
        lax.psum_scatter(d_norm_gain, ("shard", "ctx"), scatter_dimension=0, tiled=True),
        lax.psum_scatter(d_w_z, ("shard", "ctx"), scatter_dimension=0, tiled=True),
        lax.psum_scatter(d_w_x, ("shard", "ctx"), scatter_dimension=0, tiled=True),
        lax.psum_scatter(d_w_bc, ("shard", "ctx"), scatter_dimension=0, tiled=True),
        lax.psum_scatter(d_w_dt, ("shard", "ctx"), scatter_dimension=0, tiled=True),
        lax.psum_scatter(d_w_out, ("shard", "ctx"), scatter_dimension=0, tiled=True),
    )
    grads_small = lax.psum(
        (
            d_conv_w[:, :inner_local],
            d_conv_b[:inner_local],
            d_conv_w[:, inner_local:],
            d_conv_b[inner_local:],
            d_dt_bias,
            d_a_log,
            d_d_skip,
            d_gate_gain,
        ),
        ("shard", "ctx"),
    )
    return (block_out, d_input) + tuple(grads_rows) + tuple(grads_small)


def solution(mesh):
    in_specs = (
        P(("shard", "ctx"), None),
        P(("shard", "ctx")),
        P(("shard", "ctx"), "tp"),
        P(("shard", "ctx"), "tp"),
        P(("shard", "ctx"), None),
        P(("shard", "ctx"), "tp"),
        P(("shard", "ctx"), "tp"),
        P(None, "tp"),
        P("tp"),
        P(),
        P(),
        P("tp"),
        P("tp"),
        P("tp"),
        P("tp"),
        P("shard", None),
        P(("shard", "ctx")),
        P(("shard", "ctx"), None),
    )
    out_specs = (
        P(("shard", "ctx"), None),
        P(("shard", "ctx"), None),
        P(("shard", "ctx")),
        P(("shard", "ctx"), "tp"),
        P(("shard", "ctx"), "tp"),
        P(("shard", "ctx"), None),
        P(("shard", "ctx"), "tp"),
        P(("shard", "ctx"), "tp"),
        P(None, "tp"),
        P("tp"),
        P(),
        P(),
        P("tp"),
        P("tp"),
        P("tp"),
        P("tp"),
    )
    return jax.shard_map(local, mesh=mesh, in_specs=in_specs, out_specs=out_specs, check_vma=False)
```

profile of v0, /device:TPU:0, one launch (start us, length us, event | category | flops | bytes accessed | tf_op | source)
XLA Modules:
  0.0 740.0 jit_solution(11802772504556796452)
XLA Ops:
  11.0 23.3 %all-reduce.10 = bf16[768]{0:T(1024)(128)(2,1)S(1)} all-reduce(bf16[768]{0:T(1024)(128)(2,1)S(1)} %dynamic-update-slice), channel_id=1, replica_groups=mesh['shard'=2,'ctx'=4,'tp'=4] {'shard','ctx'}, use_global_device_ids=true, to_apply=%add.10 | all-reduce | flops 768 | bytes 3072
  36.5 33.1 %all_gather.19 = bf16[768,384]{1,0:T(8,128)(2,1)S(1)} all-gather(bf16[96,384]{1,0:T(8,128)(2,1)} %param.25), channel_id=1, replica_groups=mesh['shard'=2,'ctx'=4,'tp'=4] {'shard','ctx'}, dimensions={0}, use_global_device_ids=true | all-gather | bytes 663552 | tf_op jit(solution)/shard_map/all_gather | solution.py:135
  69.5 31.4 %all_gather.40 = bf16[768,256]{1,0:T(8,128)(2,1)S(1)} all-gather(bf16[96,256]{1,0:T(8,128)(2,1)S(1)} %copy-done.60), channel_id=1, replica_groups=mesh['shard'=2,'ctx'=4,'tp'=4] {'shard','ctx'}, dimensions={0}, use_global_device_ids=true | all-gather | bytes 442368 | tf_op jit(solution)/shard_map/all_gather | solution.py:136
  105.3 27.0 %all-gather = bf16[8,96,6]{1,2,0:T(8,128)(2,1)S(1)} all-gather(bf16[1,96,6]{1,2,0:T(8,128)(2,1)S(1)} %bitcast.232), channel_id=1, replica_groups=mesh['shard'=2,'ctx'=4,'tp'=4] {'shard','ctx'}, dimensions={0}, use_global_device_ids=true | all-gather | bytes 10368 | tf_op jit(solution)/shard_map/all_gather | solution.py:137
  133.6 3.6 reduce-window.30
  140.0 34.6 %all_gather.44 = bf16[768,384]{1,0:T(8,128)(2,1)} all-gather(bf16[96,384]{1,0:T(8,128)(2,1)S(1)} %copy-done.49), channel_id=1, replica_groups=mesh['shard'=2,'ctx'=4,'tp'=4] {'shard','ctx'}, dimensions={0}, use_global_device_ids=true | all-gather | bytes 663552 | tf_op jit(solution)/shard_map/all_gather | solution.py:134
  174.6 34.8 %all_gather.45 = bf16[768,384]{1,0:T(8,128)(2,1)} all-gather(bf16[96,384]{1,0:T(8,128)(2,1)S(1)} %copy-done.50), channel_id=1, replica_groups=mesh['shard'=2,'ctx'=4,'tp'=4] {'shard','ctx'}, dimensions={0}, use_global_device_ids=true | all-gather | bytes 663552 | tf_op jit(solution)/shard_map/all_gather | solution.py:138
  209.5 7.8 %all-gather.1 = f32[4,1,6]{2,1,0:T(1,128)} all-gather(f32[1,1,6]{2,1,0:T(1,128)S(1)} %get-tuple-element.329), channel_id=1, replica_groups=mesh['shard'=2,'ctx'=4,'tp'=4] {'ctx'}, dimensions={0}, use_global_device_ids=true | all-gather | bytes 120 | tf_op jit(solution)/shard_map/all_gather | solution.py:20
  232.5 16.5 %all_gather.43 = f32[4,6,64,128]{3,2,1,0:T(8,128)} all-gather(f32[1,6,64,128]{3,2,1,0:T(8,128)S(1)} %slice_add_fusion.2), channel_id=1, replica_groups=mesh['shard'=2,'ctx'=4,'tp'=4] {'ctx'}, dimensions={0}, use_global_device_ids=true | all-gather | bytes 983040 | tf_op jit(solution)/shard_map/all_gather | solution.py:20
  258.5 4.0 fusion.35
  265.5 5.6 psum.91
  271.1 3.6 multiply_reduce_fusion.8
  274.7 6.7 psum.93
  281.4 4.0 multiply_reduce_fusion.9
  290.3 6.0 fusion.9
  297.2 23.9 %all_gather.46 = f32[4,6,64,128]{3,2,1,0:T(8,128)} all-gather(f32[1,6,64,128]{3,2,1,0:T(8,128)S(1)} %slice_add_fusion.1), channel_id=1, replica_groups=mesh['shard'=2,'ctx'=4,'tp'=4] {'ctx'}, dimensions={0}, use_global_device_ids=true | all-gather | bytes 983040 | tf_op jit(solution)/shard_map/all_gather | solution.py:20
  321.2 5.4 while.27
  328.4 2.9 multiply_reduce_fusion.10
  338.9 15.8 %reduce-window.34 = f32[2,6,2,128]{3,2,1,0:T(2,128)S(1)} reduce-window(f32[2,6,2,128]{3,2,1,0:T(2,128)} %reshape.371, f32[]{:T(128)} %constant.100.clone.1), window={size=1x1x1x128 pad=0_0x0_0x0_0x0_127}, to_apply=%region_20.21 | reduce-window | flops 390144 | bytes 24580 | tf_op jit(solution)/shard_map/reduce-window.3
  365.3 15.1 %reduce-window.43 = f32[2,6,2,128]{3,2,1,0:T(2,128)S(1)} reduce-window(f32[2,6,2,128]{3,2,1,0:T(2,128)S(1)} %reshape.373, f32[]{:T(128)} %constant.100.clone.1), window={size=1x1x1x128 pad=0_0x0_0x0_0x0_127}, to_apply=%region_26.27 | reduce-window | flops 390144 | bytes 24580 | tf_op jit(solution)/shard_map/reduce-window.5
  381.4 4.2 fusion.32
  403.0 23.9 %all-reduce.17.cloned.1.call-done = f32[512,256]{0,1:T(8,128)} async-done(((f32[512,256]{0,1:T(8,128)}), f32[512,256]{0,1:T(8,128)}) %all-reduce.17.cloned.1.call-update) | async-done | bytes 524304 | tf_op jit(solution)/shard_map/psum | solution.py:265
  427.0 4.1 multiply_reduce_fusion.7
  434.4 7.6 %collective-permute-done.1 = f32[3,640]{0,1:T(8,128)S(1)} collective-permute-done((f32[3,640]{0,1:T(8,128)S(1)}, f32[3,640]{0,1:T(8,128)S(1)}, u32[]{:S(2)}, u32[]{:S(2)}) %collective-permute-start.1) | collective-permute-done | bytes 7712 | tf_op jit(solution)/shard_map/ppermute | solution.py:13
  450.3 3.0 copy.363
  457.8 4.8 reduce-scatter.16.cloned.1.call-done
  464.3 50.1 %all-reduce.19.cloned.1.call-done = (f32[512,768]{1,0:T(8,128)}, f32[512,768]{1,0:T(8,128)}) async-done(((f32[512,768]{1,0:T(8,128)}, f32[512,768]{1,0:T(8,128)}), (f32[512,768]{1,0:T(8,128)}, f32[512,768]{1,0:T(8,128)})) %all-reduce.19.cloned.1.call-update) | async-done | bytes 3145744 | tf_op jit(solution)/shard_map/psum | solution.py:215
  516.2 37.9 %all-reduce.12 = (f32[768]{0:T(1024)S(1)}, f32[4,384]{1,0:T(4,128)}, f32[384]{0:T(512)}, f32[4,256]{1,0:T(4,128)}, f32[256]{0:T(256)}, /*index=5*/f32[6]{0:T(128)}, f32[6]{0:T(128)}, f32[6]{0:T(128)}, f32[384]{0:T(512)}) all-reduce(f32[768]{0:T(1024)S(1)} %get-tuple-element.246, ...), channel_id=2, replica_groups=mesh['shard'=2,'ctx'=4,'tp'=4] {'shard','ctx'}, use_global_device_ids=true, to_apply=%region_31.32.clone | all-reduce | flops 4370 | bytes 34960
  554.7 4.5 multiply_subtract_fusion
  559.3 37.2 %reduce-scatter.18.cloned.1.call-done = f32[96,384]{1,0:T(8,128)} async-done(((f32[768,384]{1,0:T(8,128)}), f32[96,384]{1,0:T(8,128)}) %reduce-scatter.18.cloned.1.call-update) | async-done | bytes 147472
  596.5 67.8 %reduce-scatter.10.cloned.1.call-done = f32[96,384]{1,0:T(8,128)} async-done(((f32[768,384]{1,0:T(8,128)}), f32[96,384]{1,0:T(8,128)}) %reduce-scatter.10.cloned.1.call-update) | async-done | bytes 147472 | tf_op jit(solution)/shard_map/reduce_scatter | solution.py:305
  664.3 67.8 %reduce-scatter.12.cloned.1.call-done = f32[96,384]{1,0:T(8,128)} async-done(((f32[768,384]{1,0:T(8,128)}), f32[96,384]{1,0:T(8,128)}) %reduce-scatter.12.cloned.1.call-update) | async-done | bytes 147472 | tf_op jit(solution)/shard_map/reduce_scatter | solution.py:306
  (408 shorter events, 108.1 us)
Async XLA Ops:
  8.0 93.0 %copy-start = (f32[512,768]{1,0:T(8,128)S(1)}, f32[512,768]{1,0:T(8,128)}, u32[]{:S(2)}) copy-start(f32[512,768]{1,0:T(8,128)} %param.22) | copy-start | bytes 4718596
  8.0 61.5 %copy-start.60 = (bf16[96,256]{1,0:T(8,128)(2,1)S(1)}, bf16[96,256]{1,0:T(8,128)(2,1)}, u32[]{:S(2)}) copy-start(bf16[96,256]{1,0:T(8,128)(2,1)} %param.26) | copy-start | bytes 147460
  8.0 418.9 %all-reduce.17.cloned.1.call-start = ((), (), s32[]{:S(2)}) async-start(), calls=%async_computation.5 | async-start | bytes 1048576 | tf_op jit(solution)/shard_map/psum | solution.py:265
  34.3 66.9 %copy-start.51 = (f32[768]{0:T(1024)}, f32[768]{0:T(1024)S(1)}, u32[]{:S(2)}) copy-start(f32[768]{0:T(1024)S(1)} %convert_element_type.71) | copy-start | bytes 9220
  36.5 64.7 %copy-start.78 = (f32[512]{0:T(512)}, f32[512]{0:T(512)S(1)}, u32[]{:S(2)}) copy-start(f32[512]{0:T(512)S(1)} %get-tuple-element.322) | copy-start | bytes 6148
  102.3 72.3 %copy-start.50 = (bf16[96,384]{1,0:T(8,128)(2,1)S(1)}, bf16[96,384]{1,0:T(8,128)(2,1)}, u32[]{:S(2)}) copy-start(bf16[96,384]{1,0:T(8,128)(2,1)} %param.28) | copy-start | bytes 221188
  102.4 107.1 %copy-start.108 = (f32[384]{0:T(512)S(1)}, f32[384]{0:T(512)}, u32[]{:S(2)}) copy-start(f32[384]{0:T(512)} %param.30) | copy-start | bytes 4612
  102.4 107.1 %copy-start.115 = (f32[256]{0:T(256)S(1)}, f32[256]{0:T(256)}, u32[]{:S(2)}) copy-start(f32[256]{0:T(256)} %param.32) | copy-start | bytes 3076
  102.4 115.0 %copy-start.116 = (f32[6]{0:T(128)S(1)}, f32[6]{0:T(128)}, u32[]{:S(2)}) copy-start(f32[6]{0:T(128)} %param.35) | copy-start | bytes 76
  102.5 115.7 %collective-permute-start = (bf16[3,640]{0,1:T(8,128)(2,1)S(1)}, bf16[3,640]{0,1:T(8,128)(2,1)S(1)}, u32[]{:S(2)}, u32[]{:S(2)}) collective-permute-start(bf16[3,640]{0,1:T(8,128)(2,1)S(1)} %pad_maximum_fusion.8), channel_id=1, source_target_pairs={{0,4},{4,8},{8,12},{1,5},{5,9},{9,13},{2,6},{6,10},{10,14},{3,7},{... | collective-permute-start | bytes 11528 | tf_op jit(solution)/shard_map/ppermute | solution.py:13
  105.3 112.8 %copy-start.84 = (f32[2,256]{1,0:T(2,128)}, f32[2,256]{1,0:T(2,128)S(1)}, u32[]{:S(2)}) copy-start(f32[2,256]{1,0:T(2,128)S(1)} %get-tuple-element.323) | copy-start | bytes 6148
  105.3 112.8 %copy-start.93 = (pred[2,256]{1,0:T(4,128)(4,1)}, pred[2,256]{1,0:T(4,128)(4,1)S(1)}, u32[]{:S(2)}) copy-start(pred[2,256]{1,0:T(4,128)(4,1)S(1)} %get-tuple-element.324) | copy-start | bytes 1540
  133.5 247.9 %copy-start.41 = (f32[512,6]{0,1:T(8,128)}, f32[512,6]{0,1:T(8,128)S(1)}, u32[]{:S(2)}) copy-start(f32[512,6]{0,1:T(8,128)S(1)} %get-tuple-element.332) | copy-start | bytes 36868
  137.8 80.3 %copy-start.80 = (f32[2,6]{1,0:T(2,128)}, f32[2,6]{1,0:T(2,128)S(1)}, u32[]{:S(2)}) copy-start(f32[2,6]{1,0:T(2,128)S(1)} %slice_reduce_fusion) | copy-start | bytes 148
  139.1 79.4 %copy-start.61 = (f32[640]{0:T(1024)}, f32[640]{0:T(1024)S(1)}, u32[]{:S(2)}) copy-start(f32[640]{0:T(1024)S(1)} %get-tuple-element.259) | copy-start | bytes 7684
  139.1 79.4 %copy-start.63 = (f32[640]{0:T(1024)}, f32[640]{0:T(1024)S(1)}, u32[]{:S(2)}) copy-start(f32[640]{0:T(1024)S(1)} %get-tuple-element.260) | copy-start | bytes 7684
  139.1 79.4 %copy-start.65 = (f32[640]{0:T(1024)}, f32[640]{0:T(1024)S(1)}, u32[]{:S(2)}) copy-start(f32[640]{0:T(1024)S(1)} %get-tuple-element.261) | copy-start | bytes 7684
  139.1 79.4 %copy-start.67 = (f32[640]{0:T(1024)}, f32[640]{0:T(1024)S(1)}, u32[]{:S(2)}) copy-start(f32[640]{0:T(1024)S(1)} %get-tuple-element.262) | copy-start | bytes 7684
  174.6 43.9 %copy-start.72 = (f32[512]{0:T(512)S(1)}, f32[512]{0:T(512)}, u32[]{:S(2)}) copy-start(f32[512]{0:T(512)} %get-tuple-element.318) | copy-start | bytes 6148
  174.6 43.9 %copy-start.74 = (f32[512]{0:T(512)S(1)}, f32[512]{0:T(512)}, u32[]{:S(2)}) copy-start(f32[512]{0:T(512)} %get-tuple-element.319) | copy-start | bytes 6148
  174.6 43.9 %copy-start.76 = (f32[512]{0:T(512)S(1)}, f32[512]{0:T(512)}, u32[]{:S(2)}) copy-start(f32[512]{0:T(512)} %get-tuple-element.320) | copy-start | bytes 6148
  335.1 46.3 %copy-start.11 = (f32[2,256,6,64]{1,0,3,2:T(2,128)S(1)}, f32[2,256,6,64]{1,0,3,2:T(2,128)}, u32[]{:S(2)}) copy-start(f32[2,256,6,64]{1,0,3,2:T(2,128)} %reshape_reshape.7) | copy-start | bytes 2359300
  396.0 66.7 %reduce-scatter.16.cloned.1.call-start = ((), (), s32[]{:S(2)}) async-start(), calls=%async_computation.9 | async-start | bytes 442368
  403.0 111.4 %all-reduce.19.cloned.1.call-start = ((), (), s32[]{:S(2)}) async-start(), calls=%async_computation.11 | async-start | bytes 6291456 | tf_op jit(solution)/shard_map/psum | solution.py:215
  431.8 10.2 %collective-permute-start.1 = (f32[3,640]{0,1:T(8,128)S(1)}, f32[3,640]{0,1:T(8,128)S(1)}, u32[]{:S(2)}, u32[]{:S(2)}) collective-permute-start(f32[3,640]{0,1:T(8,128)S(1)} %pad_add_fusion.1), channel_id=1, source_target_pairs={{4,0},{8,4},{12,8},{5,1},{9,5},{13,9},{6,2},{10,6},{14,10},{7,3},{... | collective-permute-start | bytes 23048 | tf_op jit(solution)/shard_map/ppermute | solution.py:13
  446.1 113.1 %reduce-scatter.14.cloned.1.call-start = ((), (), s32[]{:S(2)}) async-start(), calls=%async_computation.8 | async-start | bytes 884736 | tf_op jit(solution)/shard_map/reduce_scatter | solution.py:307
  448.6 147.9 %reduce-scatter.18.cloned.1.call-start = ((), (), s32[]{:S(2)}) async-start(), calls=%async_computation.10 | async-start | bytes 1327104
  453.3 211.0 %reduce-scatter.10.cloned.1.call-start = ((), (), s32[]{:S(2)}) async-start(), calls=%async_computation.6 | async-start | bytes 1327104 | tf_op jit(solution)/shard_map/reduce_scatter | solution.py:305
  455.1 59.2 %copy-start.1 = (f32[512,768]{1,0:T(8,128)S(1)}, f32[512,768]{1,0:T(8,128)}, u32[]{:S(2)}) copy-start(f32[512,768]{1,0:T(8,128)} %param.22) | copy-start | bytes 4718596
  455.2 59.2 %copy-start.52 = (f32[768]{0:T(1024)S(1)}, f32[768]{0:T(1024)}, u32[]{:S(2)}) copy-start(f32[768]{0:T(1024)} %copy-done.51) | copy-start | bytes 9220
  455.2 59.2 %copy-start.79 = (f32[512]{0:T(512)S(1)}, f32[512]{0:T(512)}, u32[]{:S(2)}) copy-start(f32[512]{0:T(512)} %copy-done.78) | copy-start | bytes 6148
  455.2 277.0 %reduce-scatter.12.cloned.1.call-start = ((), (), s32[]{:S(2)}) async-start(), calls=%async_computation.7 | async-start | bytes 1327104 | tf_op jit(solution)/shard_map/reduce_scatter | solution.py:306
  (98 other events, 854.0 us)
Sparse Core Ops, SparseCore 0:
  396.1 30.8 all-reduce.16
  446.2 68.0 all-reduce.18
Sparse Core Ops, SparseCore 1:
  403.0 59.5 reduce-scatter.15
  466.4 62.3 reduce-scatter.13
  532.6 63.8 reduce-scatter.17
  600.5 63.8 reduce-scatter.9
  668.3 63.8 reduce-scatter.11
where the time goes:
time: 747 us; the launch traced here: 740 us
  blocking collectives  283 us (38%)
  waiting for transfers between devices  259 us (35%)
  other arithmetic  79.2 us (11%)
  matrix products  52.3 us (7%)
  local copies, waits for them, and re-layouts  43.6 us (6%)
  between operations  18.8 us (3%)
    reduce_scatter x1, waiting for transfers between devices, local(): lax.psum_scatter(d_w_x, ('shard', 'ctx'), scatter_dimension=0, tiled=True)  67.8 us
    reduce_scatter x1, waiting for transfers between devices, local(): lax.psum_scatter(d_w_z, ('shard', 'ctx'), scatter_dimension=0, tiled=True)  67.8 us
    unnamed x2, blocking collectives  61.2 us
    psum x1, waiting for transfers between devices, local(): block_out = x_in + lax.psum(contract_cols(mixed, wout_all), 'tp')  50.1 us
    all_gather x3, blocking collectives, entering_2(): gathered = jax.tree.map(lambda a: lax.all_gather(a, axis), part)  48.2 us
    unnamed x9, waiting for transfers between devices  42.1 us
    another operation x12, other arithmetic  38.2 us
    all_gather x1, blocking collectives, local(): lax.all_gather(w_out, ('shard', 'ctx'), axis=0, tiled=True)  34.8 us
  transfers between devices with their start and end apart: 9, of which 7 were waited for; matrix products, arithmetic and copies ran while one was open for 6% of the time, Pallas kernels for 0%

commit v1 on v0

--- a/solution.py
+++ b/solution.py
@@ -212,7 +212,11 @@
     square_sum = lax.psum(jnp.sum(gated * gated, axis=1), "tp")
     inv_gate = lax.rsqrt(square_sum / inner_total + norm_eps)
     mixed = (gated * inv_gate[:, None] * gate_gain[None, :]).astype(jnp.bfloat16)
-    block_out = x_in + lax.psum(contract_cols(mixed, wout_all), "tp")
+
+    def read_the_object(t0):
+        return jnp.sum(lax.all_gather(t0, axis_name="tp"), axis=0)
+
+    block_out = x_in + read_the_object(contract_cols(mixed, wout_all))
     weights_back = (
         lax.all_gather(norm_gain, ("shard", "ctx"), axis=0, tiled=True),
         lax.all_gather(w_z, ("shard", "ctx"), axis=0, tiled=True),

time: 747 us -> 722 us (0.967)
  local copies, waits for them, and re-layouts: 43.6 us -> 26.7 us
    unnamed x9 -> x10, waiting for transfers between devices: 42.1 us -> 95.1 us
    psum x1, waiting for transfers between devices: 50.1 us -> 0.02 us  [local(): d_normed = lax.psum(d_normed_part, 'tp')]
    psum x1, waiting for transfers between devices: 23.9 us -> 0.02 us  [local(): lax.psum(jnp.concatenate([(g_b + s_b).reshape(row_count, state_width), g_...]
    reduce_scatter x1, waiting for transfers between devices: 0.01 us -> 8.76 us  [local(): lax.psum_scatter(d_w_bc, ('shard', 'ctx'), scatter_dimension=0, tiled=True)]
    all_gather x0 -> x1, waiting for transfers between devices: none -> 8.21 us  [read_the_object(): return jnp.sum(lax.all_gather(t0, axis_name='tp'), axis=0)]
  transfers between devices with their start and end apart: 9 -> 10, of which waited for: 7 -> 7; matrix products, arithmetic and copies ran while one was open for 6% -> 12% of each run, Pallas kernels for 0% -> 0%
where the time goes in v1:
time: 722 us; the launch traced here: 715 us
  blocking collectives  279 us (39%)
  waiting for transfers between devices  254 us (35%)
  other arithmetic  77.3 us (11%)
  matrix products  55.1 us (8%)
  local copies, waits for them, and re-layouts  26.7 us (4%)
  between operations  18.6 us (3%)
    unnamed x10, waiting for transfers between devices  95.1 us
    reduce_scatter x1, waiting for transfers between devices, local(): lax.psum_scatter(d_w_x, ('shard', 'ctx'), scatter_dimension=0, tiled=True)  67.7 us
    reduce_scatter x1, waiting for transfers between devices, local(): lax.psum_scatter(d_w_z, ('shard', 'ctx'), scatter_dimension=0, tiled=True)  67.6 us
    unnamed x2, blocking collectives  57.6 us
    all_gather x3, blocking collectives, entering_2(): gathered = jax.tree.map(lambda a: lax.all_gather(a, axis), part)  45.6 us
    all_gather x1, blocking collectives, local(): lax.all_gather(w_z, ('shard', 'ctx'), axis=0, tiled=True)  34.9 us
    another operation x12, other arithmetic  34.9 us
    all_gather x1, blocking collectives, local(): lax.all_gather(w_out, ('shard', 'ctx'), axis=0, tiled=True)  34.7 us
  transfers between devices with their start and end apart: 10, of which 7 were waited for; matrix products, arithmetic and copies ran while one was open for 12% of the time, Pallas kernels for 0%

profile of v1, /device:TPU:0, one launch (start us, length us, event | category | flops | bytes accessed | tf_op | source)
XLA Modules:
  0.0 714.8 jit_solution(2781560469763815800)
XLA Ops:
  8.1 34.0 %all_gather.46 = bf16[768,256]{1,0:T(8,128)(2,1)S(1)} all-gather(bf16[96,256]{1,0:T(8,128)(2,1)} %param.26), channel_id=1, replica_groups=mesh['shard'=2,'ctx'=4,'tp'=4] {'shard','ctx'}, dimensions={0}, use_global_device_ids=true | all-gather | bytes 442368 | tf_op jit(solution)/shard_map/all_gather | solution.py:136
  44.9 21.6 %all-reduce.10 = bf16[768]{0:T(1024)(128)(2,1)S(1)} all-reduce(bf16[768]{0:T(1024)(128)(2,1)S(1)} %dynamic-update-slice), channel_id=1, replica_groups=mesh['shard'=2,'ctx'=4,'tp'=4] {'shard','ctx'}, use_global_device_ids=true, to_apply=%add.10 | all-reduce | flops 768 | bytes 3072
  68.7 32.2 %all_gather.45 = bf16[768,384]{1,0:T(8,128)(2,1)S(1)} all-gather(bf16[96,384]{1,0:T(8,128)(2,1)S(1)} %copy-done.47), channel_id=1, replica_groups=mesh['shard'=2,'ctx'=4,'tp'=4] {'shard','ctx'}, dimensions={0}, use_global_device_ids=true | all-gather | bytes 663552 | tf_op jit(solution)/shard_map/all_gather | solution.py:135
  105.4 27.1 %all-gather.1 = bf16[8,96,6]{1,2,0:T(8,128)(2,1)S(1)} all-gather(bf16[1,96,6]{1,2,0:T(8,128)(2,1)S(1)} %bitcast.234), channel_id=1, replica_groups=mesh['shard'=2,'ctx'=4,'tp'=4] {'shard','ctx'}, dimensions={0}, use_global_device_ids=true | all-gather | bytes 10368 | tf_op jit(solution)/shard_map/all_gather | solution.py:137
  133.6 3.6 reduce-window.30
  139.9 34.9 %all_gather.50 = bf16[768,384]{1,0:T(8,128)(2,1)} all-gather(bf16[96,384]{1,0:T(8,128)(2,1)S(1)} %copy-done.48), channel_id=1, replica_groups=mesh['shard'=2,'ctx'=4,'tp'=4] {'shard','ctx'}, dimensions={0}, use_global_device_ids=true | all-gather | bytes 663552 | tf_op jit(solution)/shard_map/all_gather | solution.py:134
  174.8 34.7 %all_gather.51 = bf16[768,384]{1,0:T(8,128)(2,1)} all-gather(bf16[96,384]{1,0:T(8,128)(2,1)S(1)} %copy-done.49), channel_id=1, replica_groups=mesh['shard'=2,'ctx'=4,'tp'=4] {'shard','ctx'}, dimensions={0}, use_global_device_ids=true | all-gather | bytes 663552 | tf_op jit(solution)/shard_map/all_gather | solution.py:138
  209.6 8.1 %all-gather.2 = f32[4,1,6]{2,1,0:T(1,128)S(1)} all-gather(f32[1,1,6]{2,1,0:T(1,128)S(1)} %get-tuple-element.327), channel_id=1, replica_groups=mesh['shard'=2,'ctx'=4,'tp'=4] {'ctx'}, dimensions={0}, use_global_device_ids=true | all-gather | bytes 120 | tf_op jit(solution)/shard_map/all_gather | solution.py:20
  230.4 16.4 %all_gather.49 = f32[4,6,64,128]{3,2,1,0:T(8,128)} all-gather(f32[1,6,64,128]{3,2,1,0:T(8,128)S(1)} %slice_add_fusion.2), channel_id=1, replica_groups=mesh['shard'=2,'ctx'=4,'tp'=4] {'ctx'}, dimensions={0}, use_global_device_ids=true | all-gather | bytes 983040 | tf_op jit(solution)/shard_map/all_gather | solution.py:20
  250.9 4.0 fusion.35
  257.8 5.6 psum.84
  263.5 3.5 multiply_reduce_fusion.8
  267.0 7.2 %psum.85 = f32[512]{0:T(512)S(1)} all-reduce(f32[512]{0:T(512)S(1)} %get-tuple-element.253), channel_id=1, replica_groups=mesh['shard'=2,'ctx'=4,'tp'=4] {'tp'}, use_global_device_ids=true, to_apply=%region_11.12 | all-reduce | flops 512 | bytes 4096 | tf_op jit(solution)/shard_map/psum | solution.py:233
  274.2 4.0 multiply_reduce_fusion.9
  284.2 7.4 %fusion.9 = (f32[2,256,6]{1,2,0:T(8,128)}, f32[2,256,6]{1,2,0:T(8,128)}, f32[2,256,6]{1,2,0:T(8,128)}, f32[2,256,256]{2,1,0:T(8,128)}) fusion(f32[2,256,6]{1,2,0:T(8,128)S(1)} %bitcast.221, f32[2,256,6]{1,2,0:T(8,128)S(1)} %bitcast.215, f32[2,256,256]{2,1,0:T(8,128)} %copy-done.40, pred[2,256,256]{2,1,0:T(8,128)(4,1)} %compare_and_fusion, ...), kind=kOutput, calls=%fused_computation.17 | convolution fusion | flops 615635968 | bytes 2813952 | tf_op jit(solution)/shard_map/transpose(jvp(vmap(tsh,shp->thp)))/dot_general | solution.py:65
  292.5 21.1 %all_gather.54 = f32[4,6,64,128]{3,2,1,0:T(8,128)} all-gather(f32[1,6,64,128]{3,2,1,0:T(8,128)S(1)} %slice_add_fusion.1), channel_id=1, replica_groups=mesh['shard'=2,'ctx'=4,'tp'=4] {'ctx'}, dimensions={0}, use_global_device_ids=true | all-gather | bytes 983040 | tf_op jit(solution)/shard_map/all_gather | solution.py:20
  313.6 3.4 while.27
  318.8 3.4 convolution_bitcast_fusion.2
  332.7 4.2 fusion.32
  339.9 15.1 %reduce-window.43 = f32[2,6,2,128]{3,2,1,0:T(2,128)S(1)} reduce-window(f32[2,6,2,128]{3,2,1,0:T(2,128)S(1)} %reshape.374, f32[]{:T(128)} %constant.100.clone.1), window={size=1x1x1x128 pad=0_0x0_0x0_0x0_127}, to_apply=%region_26.27 | reduce-window | flops 390144 | bytes 24580 | tf_op jit(solution)/shard_map/reduce-window.5
  356.2 15.1 %reduce-window.34 = f32[2,6,2,128]{3,2,1,0:T(2,128)S(1)} reduce-window(f32[2,6,2,128]{3,2,1,0:T(2,128)S(1)} %reshape.372, f32[]{:T(128)} %constant.100.clone.1), window={size=1x1x1x128 pad=0_0x0_0x0_0x0_127}, to_apply=%region_20.21 | reduce-window | flops 390144 | bytes 24580 | tf_op jit(solution)/shard_map/reduce-window.3
  378.7 4.0 multiply_reduce_fusion.7
  386.1 7.0 collective-permute-done.1
  410.7 27.3 %reduce-scatter.16.cloned.1.call-done = f32[96,6]{1,0:T(8,128)} async-done(((f32[768,6]{1,0:T(8,128)}), f32[96,6]{1,0:T(8,128)}) %reduce-scatter.16.cloned.1.call-update) | async-done | bytes 2320
  441.6 36.0 %all-reduce.12 = (f32[768]{0:T(1024)S(1)}, f32[4,384]{1,0:T(4,128)}, f32[384]{0:T(512)}, f32[4,256]{1,0:T(4,128)}, f32[256]{0:T(256)}, /*index=5*/f32[6]{0:T(128)}, f32[6]{0:T(128)}, f32[6]{0:T(128)}, f32[384]{0:T(512)}) all-reduce(f32[768]{0:T(1024)S(1)} %get-tuple-element.246, ...), channel_id=3, replica_groups=mesh['shard'=2,'ctx'=4,'tp'=4] {'shard','ctx'}, use_global_device_ids=true, to_apply=%region_31.32.clone | all-reduce | flops 4370 | bytes 34960
  478.2 8.2 %all-gather.5.cloned.1.call-done = f32[2048,768]{1,0:T(8,128)} async-done(((f32[512,768]{1,0:T(8,128)}), f32[2048,768]{1,0:T(8,128)}) %all-gather.5.cloned.1.call-update) | async-done | bytes 6291472 | tf_op jit(solution)/shard_map/all_gather | solution.py:217
  486.4 4.5 reduce_sum.247
  490.9 4.5 multiply_subtract_fusion
  495.5 8.8 %reduce-scatter.14.cloned.1.call-done = f32[96,256]{1,0:T(8,128)} async-done(((f32[768,256]{1,0:T(8,128)}), f32[96,256]{1,0:T(8,128)}) %reduce-scatter.14.cloned.1.call-update) | async-done | bytes 98320 | tf_op jit(solution)/shard_map/reduce_scatter | solution.py:311
  504.2 67.6 %reduce-scatter.10.cloned.1.call-done = f32[96,384]{1,0:T(8,128)} async-done(((f32[768,384]{1,0:T(8,128)}), f32[96,384]{1,0:T(8,128)}) %reduce-scatter.10.cloned.1.call-update) | async-done | bytes 147472 | tf_op jit(solution)/shard_map/reduce_scatter | solution.py:309
  571.8 67.7 %reduce-scatter.18.cloned.1.call-done = f32[96,384]{1,0:T(8,128)} async-done(((f32[768,384]{1,0:T(8,128)}), f32[96,384]{1,0:T(8,128)}) %reduce-scatter.18.cloned.1.call-update) | async-done | bytes 147472
  639.5 67.7 %reduce-scatter.12.cloned.1.call-done = f32[96,384]{1,0:T(8,128)} async-done(((f32[768,384]{1,0:T(8,128)}), f32[96,384]{1,0:T(8,128)}) %reduce-scatter.12.cloned.1.call-update) | async-done | bytes 147472 | tf_op jit(solution)/shard_map/reduce_scatter | solution.py:310
  (396 shorter events, 89.4 us)
Async XLA Ops:
  8.0 92.8 %copy-start = (f32[512,768]{1,0:T(8,128)S(1)}, f32[512,768]{1,0:T(8,128)}, u32[]{:S(2)}) copy-start(f32[512,768]{1,0:T(8,128)} %param.22) | copy-start | bytes 4718596
  8.0 60.6 %copy-start.47 = (bf16[96,384]{1,0:T(8,128)(2,1)S(1)}, bf16[96,384]{1,0:T(8,128)(2,1)}, u32[]{:S(2)}) copy-start(bf16[96,384]{1,0:T(8,128)(2,1)} %param.25) | copy-start | bytes 221188
  8.0 370.6 %all-reduce.16.cloned.1.call-start = ((), (), s32[]{:S(2)}) async-start(), calls=%async_computation.5 | async-start | bytes 1048576 | tf_op jit(solution)/shard_map/psum | solution.py:269
  42.0 59.0 %copy-start.25 = (bf16[768,256]{1,0:T(8,128)(2,1)}, bf16[768,256]{1,0:T(8,128)(2,1)S(1)}, u32[]{:S(2)}) copy-start(bf16[768,256]{1,0:T(8,128)(2,1)S(1)} %all_gather.46) | copy-start | bytes 1179652
  102.3 37.6 %copy-start.48 = (bf16[96,384]{1,0:T(8,128)(2,1)S(1)}, bf16[96,384]{1,0:T(8,128)(2,1)}, u32[]{:S(2)}) copy-start(bf16[96,384]{1,0:T(8,128)(2,1)} %param.24) | copy-start | bytes 221188
  102.3 72.5 %copy-start.49 = (bf16[96,384]{1,0:T(8,128)(2,1)S(1)}, bf16[96,384]{1,0:T(8,128)(2,1)}, u32[]{:S(2)}) copy-start(bf16[96,384]{1,0:T(8,128)(2,1)} %param.28) | copy-start | bytes 221188
  102.4 107.2 %copy-start.101 = (f32[384]{0:T(512)S(1)}, f32[384]{0:T(512)}, u32[]{:S(2)}) copy-start(f32[384]{0:T(512)} %param.30) | copy-start | bytes 4612
  102.4 107.2 %copy-start.107 = (f32[256]{0:T(256)S(1)}, f32[256]{0:T(256)}, u32[]{:S(2)}) copy-start(f32[256]{0:T(256)} %param.32) | copy-start | bytes 3076
  102.4 115.3 %copy-start.108 = (f32[6]{0:T(128)S(1)}, f32[6]{0:T(128)}, u32[]{:S(2)}) copy-start(f32[6]{0:T(128)} %param.35) | copy-start | bytes 76
  102.5 115.4 %collective-permute-start = (bf16[3,640]{0,1:T(8,128)(2,1)S(1)}, bf16[3,640]{0,1:T(8,128)(2,1)S(1)}, u32[]{:S(2)}, u32[]{:S(2)}) collective-permute-start(bf16[3,640]{0,1:T(8,128)(2,1)S(1)} %pad_maximum_fusion.8), channel_id=1, source_target_pairs={{0,4},{4,8},{8,12},{1,5},{5,9},{9,13},{2,6},{6,10},{10,14},{3,7},{... | collective-permute-start | bytes 11528 | tf_op jit(solution)/shard_map/ppermute | solution.py:13
  105.3 112.5 %copy-start.78 = (f32[2,256]{1,0:T(2,128)}, f32[2,256]{1,0:T(2,128)S(1)}, u32[]{:S(2)}) copy-start(f32[2,256]{1,0:T(2,128)S(1)} %get-tuple-element.321) | copy-start | bytes 6148
  105.3 112.5 %copy-start.85 = (pred[2,256]{1,0:T(4,128)(4,1)}, pred[2,256]{1,0:T(4,128)(4,1)S(1)}, u32[]{:S(2)}) copy-start(pred[2,256]{1,0:T(4,128)(4,1)S(1)} %get-tuple-element.322) | copy-start | bytes 1540
  105.4 104.1 %copy-start.94 = (f32[2]{0:T(128)}, f32[2]{0:T(128)S(1)}, u32[]{:S(2)}) copy-start(f32[2]{0:T(128)S(1)} %compare_convert_fusion.1) | copy-start | bytes 28
  132.6 85.3 %copy-start.45 = (bf16[768,6]{0,1:T(8,128)(2,1)}, bf16[768,6]{0,1:T(8,128)(2,1)S(1)}, u32[]{:S(2)}) copy-start(bf16[768,6]{0,1:T(8,128)(2,1)S(1)} %reshape.360) | copy-start | bytes 27652
  133.5 199.2 %copy-start.41 = (f32[512,6]{0,1:T(8,128)}, f32[512,6]{0,1:T(8,128)S(1)}, u32[]{:S(2)}) copy-start(f32[512,6]{0,1:T(8,128)S(1)} %get-tuple-element.330) | copy-start | bytes 36868
  137.9 80.0 %copy-start.74 = (f32[2,6]{1,0:T(2,128)}, f32[2,6]{1,0:T(2,128)S(1)}, u32[]{:S(2)}) copy-start(f32[2,6]{1,0:T(2,128)S(1)} %slice_reduce_fusion) | copy-start | bytes 148
  139.0 79.2 %copy-start.56 = (f32[640]{0:T(1024)}, f32[640]{0:T(1024)S(1)}, u32[]{:S(2)}) copy-start(f32[640]{0:T(1024)S(1)} %get-tuple-element.259) | copy-start | bytes 7684
  139.0 79.2 %copy-start.58 = (f32[640]{0:T(1024)}, f32[640]{0:T(1024)S(1)}, u32[]{:S(2)}) copy-start(f32[640]{0:T(1024)S(1)} %get-tuple-element.260) | copy-start | bytes 7684
  139.0 79.2 %copy-start.60 = (f32[640]{0:T(1024)}, f32[640]{0:T(1024)S(1)}, u32[]{:S(2)}) copy-start(f32[640]{0:T(1024)S(1)} %get-tuple-element.261) | copy-start | bytes 7684
  139.1 79.2 %copy-start.62 = (f32[640]{0:T(1024)}, f32[640]{0:T(1024)S(1)}, u32[]{:S(2)}) copy-start(f32[640]{0:T(1024)S(1)} %get-tuple-element.262) | copy-start | bytes 7684
  174.8 43.5 %copy-start.66 = (f32[512]{0:T(512)S(1)}, f32[512]{0:T(512)}, u32[]{:S(2)}) copy-start(f32[512]{0:T(512)} %get-tuple-element.316) | copy-start | bytes 6148
  174.8 43.5 %copy-start.68 = (f32[512]{0:T(512)S(1)}, f32[512]{0:T(512)}, u32[]{:S(2)}) copy-start(f32[512]{0:T(512)} %get-tuple-element.317) | copy-start | bytes 6148
  174.8 43.5 %copy-start.70 = (f32[512]{0:T(512)S(1)}, f32[512]{0:T(512)}, u32[]{:S(2)}) copy-start(f32[512]{0:T(512)} %get-tuple-element.318) | copy-start | bytes 6148
  217.9 56.4 %copy-start.80 = (f32[384]{0:T(512)}, f32[384]{0:T(512)S(1)}, u32[]{:S(2)}) copy-start(f32[384]{0:T(512)S(1)} %mul.676) | copy-start | bytes 4612
  332.6 105.4 %reduce-scatter.16.cloned.1.call-start = ((), (), s32[]{:S(2)}) async-start(), calls=%async_computation.11 | async-start | bytes 442368
  378.3 61.3 %all-reduce.18.cloned.1.call-start = ((), (), s32[]{:S(2)}) async-start(), calls=%async_computation.6 | async-start | bytes 3145728 | tf_op jit(solution)/shard_map/psum | solution.py:299
  383.4 9.6 %collective-permute-start.1 = (f32[3,640]{0,1:T(8,128)S(1)}, f32[3,640]{0,1:T(8,128)S(1)}, u32[]{:S(2)}, u32[]{:S(2)}) collective-permute-start(f32[3,640]{0,1:T(8,128)S(1)} %pad_add_fusion.1), channel_id=1, source_target_pairs={{4,0},{8,4},{12,8},{5,1},{9,5},{13,9},{6,2},{10,6},{14,10},{7,3},{... | collective-permute-start | bytes 23048 | tf_op jit(solution)/shard_map/ppermute | solution.py:13
  397.2 89.1 %all-gather.5.cloned.1.call-start = ((), (), s32[]{:S(2)}) async-start(), calls=%async_computation.10 | async-start | bytes 7864320 | tf_op jit(solution)/shard_map/all_gather | solution.py:217
  400.4 103.8 %reduce-scatter.14.cloned.1.call-start = ((), (), s32[]{:S(2)}) async-start(), calls=%async_computation.9 | async-start | bytes 884736 | tf_op jit(solution)/shard_map/reduce_scatter | solution.py:311
  401.8 170.0 %reduce-scatter.10.cloned.1.call-start = ((), (), s32[]{:S(2)}) async-start(), calls=%async_computation.7 | async-start | bytes 1327104 | tf_op jit(solution)/shard_map/reduce_scatter | solution.py:309
  403.6 235.9 %reduce-scatter.18.cloned.1.call-start = ((), (), s32[]{:S(2)}) async-start(), calls=%async_computation.12 | async-start | bytes 1327104
  408.1 299.1 %reduce-scatter.12.cloned.1.call-start = ((), (), s32[]{:S(2)}) async-start(), calls=%async_computation.8 | async-start | bytes 1327104 | tf_op jit(solution)/shard_map/reduce_scatter | solution.py:310
  (91 other events, 905.7 us)
Sparse Core Ops, SparseCore 0:
  332.7 30.6 all-reduce.15
  397.4 40.3 all-reduce.17
  439.9 46.4 all-gather.4
Sparse Core Ops, SparseCore 1:
  378.4 59.5 reduce-scatter.15
  441.7 62.4 reduce-scatter.13
  508.0 63.7 reduce-scatter.9
  575.8 63.7 reduce-scatter.17
  643.5 63.6 reduce-scatter.11
